TPU v7x, 32 devices: a whole 2x2x4 slice. The times are simulated.
32 devices in a mesh: groups: 2 (over y), expert: 4 (over z), token: 4 (over x, core).
Axes of the slice: x: 2, y: 2, z: 4, core: 2. Of those that a mesh axis runs over, the one named last changes fastest.
Arguments:
- tokens: bfloat16 [512, 2048], P(('groups', 'expert'), 'token'), parts along dimension 0, may hold values from -6 to 6
- expert_ids: int32 [512, 8], P(('groups', 'expert')), parts along dimension 0, may hold values from 0 to 15, all different within a row; in each aligned block of 64 rows (0 to 63, 64 to 127, ...) at most 64 rows name the same one
- route_weights: float32 [512, 8], P(('groups', 'expert')), parts along dimension 0, may hold values from 0.1 to 0.4
- w_gate_up: bfloat16 [16, 2048, 1536], P('expert', 'token'), may hold values from -0.125 to 0.125
- w_down: bfloat16 [16, 768, 2048], P('expert', None, 'token'), may hold values from -0.21875 to 0.21875
Outputs:
- combined: bfloat16 [512, 2048], P(('groups', 'expert'), 'token'), parts along dimension 0
There are 2 independent parts, one for each index of `groups`. A program takes and returns all parts, laid end to end along the dimension named above; an argument that names none is the same for every part. Nothing has to cross between parts.
Inputs may be any that keep to these rules, and one draw needn't show every extreme that they name: `expert_ids`: each row names 8 different experts. In each aligned block of 64 rows no expert is named by more than 64 rows, a bound that some block reaches.
All inputs are finite; a program needn't handle non-finite values.
Results may differ from a plain program's by a relative error of at most 0.02.
Values may be sent and summed in bfloat16 or wider, within the bound.
A program may use at most 64 MiB of HBM per device.

v0:
```python
import jax
import jax.numpy as jnp
from jax import lax
from jax.sharding import PartitionSpec as P


def rank_slots(flat_ids, experts):
    onehot = (flat_ids[:, None] == jnp.arange(experts, dtype=jnp.int32)[None, :]).astype(jnp.int32)
    rank_of = jnp.sum((jnp.cumsum(onehot, axis=0) - 1) * onehot, axis=1)
    return (onehot, rank_of)


def gate_up_terms(inputs, w_gate_up):
    return jnp.einsum("erd,edf->ref", inputs, w_gate_up, preferred_element_type=jnp.float32)


def expert_block(inputs, gate_up_w, down_w):
    hidden_units = gate_up_w.shape[2] // 2
    summed = lax.psum_scatter(
        gate_up_terms(inputs, gate_up_w).astype(jnp.bfloat16),
        "token",
        scatter_dimension=0,
        tiled=True,
    ).astype(jnp.float32)
    hidden = (jax.nn.silu(summed[..., :hidden_units]) * summed[..., hidden_units:]).astype(
        jnp.bfloat16
    )
    produced = jnp.einsum(
        "reh,ehd->erd",
        lax.all_gather(hidden, "token", axis=0, tiled=True),
        down_w,
        preferred_element_type=jnp.float32,
    )
    return produced.astype(jnp.bfloat16)


def per_device(tokens, expert_ids, route_weights, w_gate_up, w_down):
    tok_dev, feature_cols = tokens.shape
    top_k = expert_ids.shape[1]
    local_experts = w_gate_up.shape[0]
    n_expert = lax.axis_size("expert")
    experts = local_experts * n_expert
    capacity = max(2, min(tok_dev, tok_dev * top_k * 5 // (2 * experts)))
    slot_count = n_expert * capacity
    flat_ids = expert_ids.reshape(-1)
    onehot, rank_of = rank_slots(flat_ids, experts)
    position = (
        flat_ids % local_experts * slot_count + flat_ids // local_experts * capacity + rank_of
    )
    token_of = jnp.arange(flat_ids.shape[0], dtype=jnp.int32) // top_k
    slot_table = (
        jnp.full((local_experts * slot_count,), tok_dev, jnp.int32).at[position].set(token_of)
    )
    padded = jnp.concatenate([tokens, jnp.zeros((1, feature_cols), tokens.dtype)], axis=0)
    outgoing = jnp.take(padded, slot_table, axis=0).reshape(
        local_experts, n_expert, capacity, feature_cols
    )
    arrived = lax.all_to_all(outgoing, "expert", split_axis=1, concat_axis=1, tiled=True)
    inputs = arrived.reshape(local_experts, slot_count, feature_cols)
    expert_out = expert_block(inputs, w_gate_up, w_down)
    returned = lax.all_to_all(
        expert_out.reshape(local_experts, n_expert, capacity, feature_cols),
        "expert",
        split_axis=1,
        concat_axis=1,
        tiled=True,
    )
    picked = jnp.take(
        returned.reshape(local_experts * slot_count, feature_cols), position, axis=0
    ).reshape(tok_dev, top_k, feature_cols)
    combined = jnp.sum(route_weights[:, :, None] * picked.astype(jnp.float32), axis=1)
    return combined.astype(jnp.bfloat16)


def solution(mesh):
    return jax.shard_map(
        per_device,
        mesh=mesh,
        in_specs=(
            P(("groups", "expert"), "token"),
            P(("groups", "expert"), None),
            P(("groups", "expert"), None),
            P("expert", "token", None),
            P("expert", None, "token"),
        ),
        out_specs=P(("groups", "expert"), "token"),
        check_vma=False,
    )
```

profile of v0, /device:TPU:0, one launch (start us, length us, event | category | flops | bytes accessed | tf_op | source)
XLA Modules:
  0.0 166.3 jit_solution(5265012218865901291)
XLA Ops:
  6.5 0.0 copy-start
  6.5 0.0 reduce-scatter.2.cloned.1.call-start
  6.5 0.9 copy.31
  7.5 0.1 eq.28
  7.6 0.1 reshape.180
  7.6 0.1 reshape.182
  7.8 1.2 reduce-window.6
  8.9 0.2 slice_reduce_fusion
  9.2 0.1 fusion.7
  9.3 2.4 %scatter_custom_fusion = s32[1024]{0:T(1024)S(1)} fusion(s32[512]{0:T(512)S(1)} %bitcast.36, s32[512]{0:T(512)S(1)} %add_select_fusion.2, s32[]{:T(128)} %constant.82.clone.1), kind=kCustom, calls=%fused_computation.54 | custom fusion | bytes 4100 | tf_op jit(solution)/shard_map/scatter | solution.py:52
  11.8 0.1 broadcast_in_dim.33
  11.9 0.8 concatenate.3
  12.7 5.1 %gather_fusion = bf16[1024,512]{1,0:T(8,128)(2,1)} fusion(bf16[65,512]{1,0:T(8,128)(2,1)S(1)} %concatenate.3, s32[1024]{0:T(1024)S(1)} %fusion.13), kind=kCustom, calls=%fused_computation | custom fusion | bytes 2101248 | tf_op jit(solution)/shard_map/jit(_take)/gather | solution.py:55
  17.8 1.4 copy_select_fusion
  19.2 31.9 %all_to_all.10 = bf16[4,4,64,512]{3,2,0,1:T(8,128)(2,1)S(1)} all-to-all(bf16[4,4,64,512]{3,2,0,1:T(8,128)(2,1)S(1)} %copy_select_fusion), channel_id=1, replica_groups=mesh['groups'=2,'expert'=4,'token'=4] {'expert'}, dimensions={1} | all-to-all | bytes 2097152 | tf_op jit(solution)/shard_map/all_to_all | solution.py:58
  51.1 0.1 copy.41
  51.2 6.3 %fusion = bf16[256,4,1536]{2,0,1:T(8,128)(2,1)} fusion(bf16[4,256,512]{2,1,0:T(8,128)(2,1)S(1)} %bitcast.33, bf16[4,512,1536]{2,1,0:T(8,128)(2,1)} %param.8), kind=kOutput, calls=%fused_computation.4 | convolution fusion | flops 1612185600 | bytes 10485760 | tf_op jit(solution)/shard_map/erd,edf->ref/dot_general | solution.py:14
  57.4 0.0 reduce-scatter.2.cloned.1.call-update
  57.5 0.0 all-gather.2.cloned.1.call-start
  57.5 37.0 %reduce-scatter.2.cloned.1.call-done = bf16[64,4,1536]{2,0,1:T(8,128)(2,1)} async-done(((bf16[256,4,1536]{2,0,1:T(8,128)(2,1)}), bf16[64,4,1536]{2,0,1:T(8,128)(2,1)}) %reduce-scatter.2.cloned.1.call-update) | async-done | bytes 786448 | tf_op jit(solution)/shard_map/reduce_scatter | solution.py:19
  94.5 1.3 convert_element_type.29
  95.8 1.0 fusion.1
  96.8 0.0 all-gather.2.cloned.1.call-update
  96.8 19.8 %all-gather.2.cloned.1.call-done = bf16[256,4,768]{2,0,1:T(8,128)(2,1)} async-done(((bf16[64,4,768]{2,0,1:T(8,128)(2,1)}), bf16[256,4,768]{2,0,1:T(8,128)(2,1)}) %all-gather.2.cloned.1.call-update) | async-done | bytes 1572880 | tf_op jit(solution)/shard_map/all_gather | solution.py:30
  116.6 0.0 copy-done
  116.6 2.4 %convolution_convert_fusion.1 = bf16[4,256,512]{2,1,0:T(8,128)(2,1)S(1)} fusion(bf16[256,4,768]{2,0,1:T(8,128)(2,1)} %all-gather.2.cloned.1.call-done, bf16[4,768,512]{2,1,0:T(8,128)(2,1)S(1)} %copy-done), kind=kOutput, calls=%fused_computation.5 | convolution fusion | flops 805830656 | bytes 5767168 | tf_op jit(solution)/shard_map/reh,ehd->erd/dot_general | solution.py:28
  119.0 0.0 copy-start.1
  119.0 1.1 copy.42
  120.1 4.6 %all-to-all-start.1 = ((bf16[4,4,64,512]{3,2,0,1:T(8,128)(2,1)}), bf16[4,4,64,512]{3,2,0,1:T(8,128)(2,1)}, u32[]{:S(2)}, u32[]{:S(2)}) async-start(bf16[4,4,64,512]{3,2,0,1:T(8,128)(2,1)} %copy.42), calls=%async_computation.2 | async-start | bytes 2097152 | tf_op jit(solution)/shard_map/all_to_all | solution.py:61
  124.7 0.1 reduce_sum.23
  124.8 0.0 copy-done.1
  124.8 0.1 copy.30
  124.9 0.1 compare_and_fusion
  125.0 26.0 %all-to-all-done.1 = bf16[4,4,64,512]{3,2,0,1:T(8,128)(2,1)} async-done(((bf16[4,4,64,512]{3,2,0,1:T(8,128)(2,1)}), bf16[4,4,64,512]{3,2,0,1:T(8,128)(2,1)}, u32[]{:S(2)}, u32[]{:S(2)}) %all-to-all-start.1) | async-done | bytes 1048608 | tf_op jit(solution)/shard_map/all_to_all | solution.py:61
  151.0 2.4 %copy.43 = bf16[4,4,64,512]{3,2,1,0:T(8,128)(2,1)} copy(bf16[4,4,64,512]{3,2,0,1:T(8,128)(2,1)} %all-to-all-done.1) | data formatting | bytes 2097152 | tf_op jit(solution)/shard_map/all_to_all | solution.py:61
  153.3 4.0 %gather_fusion.1 = bf16[512,512]{1,0:T(8,128)(2,1)} fusion(bf16[1024,512]{1,0:T(8,128)(2,1)} %bitcast.31, s32[1024]{0:T(1024)S(1)} %pad_clamp_fusion), kind=kCustom, calls=%fused_computation.1 | custom fusion | bytes 1050624 | tf_op jit(solution)/shard_map/jit(_take)/gather | solution.py:68
  157.3 2.1 %multiply_reduce_fusion = bf16[64,512]{1,0:T(8,128)(2,1)} fusion(bf16[512,512]{1,0:T(8,128)(2,1)} %gather_fusion.1, f32[64,8]{1,0:T(8,128)S(1)} %copy.30, pred[64,8]{1,0:T(8,128)(4,1)S(1)} %compare_and_fusion), kind=kLoop, calls=%fused_computation.7 | loop fusion | flops 1015808 | bytes 592384 | tf_op jit(solution)/shard_map/reduce_sum | solution.py:71
  (9 shorter events, 0.1 us)
Async XLA Ops:
  6.5 110.1 %copy-start = (bf16[4,768,512]{2,1,0:T(8,128)(2,1)S(1)}, bf16[4,768,512]{2,1,0:T(8,128)(2,1)}, u32[]{:S(2)}) copy-start(bf16[4,768,512]{2,1,0:T(8,128)(2,1)} %param.9) | copy-start | bytes 9437188
  6.5 88.0 %reduce-scatter.2.cloned.1.call-start = ((), (), s32[]{:S(2)}) async-start(), calls=%async_computation.3 | async-start | bytes 3932160 | tf_op jit(solution)/shard_map/reduce_scatter | solution.py:19
  57.5 59.1 %all-gather.2.cloned.1.call-start = ((), (), s32[]{:S(2)}) async-start(), calls=%async_computation.4 | async-start | bytes 1966080 | tf_op jit(solution)/shard_map/all_gather | solution.py:30
  119.0 5.8 %copy-start.1 = (f32[64,8]{0,1:T(8,128)S(1)}, f32[64,8]{0,1:T(8,128)}, u32[]{:S(2)}) copy-start(f32[64,8]{0,1:T(8,128)} %param.7) | copy-start | bytes 6148
  120.1 30.8 %all-to-all-start.1 = ((bf16[4,4,64,512]{3,2,0,1:T(8,128)(2,1)}), bf16[4,4,64,512]{3,2,0,1:T(8,128)(2,1)}, u32[]{:S(2)}, u32[]{:S(2)}) async-start(bf16[4,4,64,512]{3,2,0,1:T(8,128)(2,1)} %copy.42), calls=%async_computation.2 | async-start | bytes 2097152 | tf_op jit(solution)/shard_map/all_to_all | solution.py:61
Sparse Core Ops, SparseCore 0:
  57.6 36.8 reduce-scatter.1
  96.9 19.6 all-gather.1
where the time goes:
time: 167 us; the launch traced here: 166 us
  waiting for transfers between devices  82.8 us (50%)
  blocking collectives  31.9 us (19%)
  local copies, waits for them, and re-layouts  17.6 us (11%)
  between operations  13.5 us (8%)
  matrix products  8.66 us (5%)
  other arithmetic  7.2 us (4%)
  starting transfers between devices  4.64 us (3%)
    reduce_scatter x1, waiting for transfers between devices, expert_block(): lax.psum_scatter(gate_up_terms(inputs, gate_up_w).astype(jnp.bfloat16), '...  37 us
    all_to_all x1, blocking collectives, per_device(): lax.all_to_all(outgoing, 'expert', split_axis=1, concat_axis=1, tiled=True)  31.9 us
    all_to_all x1, waiting for transfers between devices, per_device(): lax.all_to_all(expert_out.reshape(local_experts, n_expert, capacity, feat...  26 us
    all_gather x1, waiting for transfers between devices, expert_block(): lax.all_gather(hidden, 'token', axis=0, tiled=True)  19.8 us
    dot_general x1, matrix products, gate_up_terms(): jnp.einsum('erd,edf->ref', inputs, w_gate_up, preferred_element_type=jnp....  6.28 us
    gather x1, local copies, waits for them, and re-layouts, per_device(): jnp.take(padded, slot_table, axis=0)  5.06 us
    all_to_all x1, starting transfers between devices, per_device(): lax.all_to_all(expert_out.reshape(local_experts, n_expert, capacity, feat...  4.6 us
    gather x1, local copies, waits for them, and re-layouts, per_device(): jnp.take(returned.reshape(local_experts * slot_count, feature_cols), posi...  4.01 us
  transfers between devices with their start and end apart: 3, of which 3 were waited for; matrix products, arithmetic and copies ran while one was open for 0% of the time, Pallas kernels for 0%

commit v1 on v0

--- a/solution.py
+++ b/solution.py
@@ -2,6 +2,28 @@
 import jax.numpy as jnp
 from jax import lax
 from jax.sharding import PartitionSpec as P
+
+
+def laid_out(blocks, dim):
+    blocks = jnp.moveaxis(blocks, 0, dim)
+    dims = blocks.shape
+    return blocks.reshape(*dims[:dim], dims[dim] * dims[dim + 1], *dims[dim + 2 :])
+
+
+def collected_by_bits(value, axis):
+    size = lax.axis_size(axis)
+    blocks = value[None]
+    for level in range(size.bit_length() - 1):
+        bit = 1 << level
+        other = lax.ppermute(blocks, axis, [(i, i ^ bit) for i in range(size)])
+        both = jnp.stack([blocks, other])
+        upper = lax.axis_index(axis) >> level & 1
+        blocks = jnp.where(upper == 0, both, both[::-1]).reshape(-1, *value.shape)
+    return blocks
+
+
+def doubled_up(value, axis, dim):
+    return laid_out(collected_by_bits(value, axis), dim)
 
 
 def rank_slots(flat_ids, experts):
@@ -26,10 +48,7 @@
         jnp.bfloat16
     )
     produced = jnp.einsum(
-        "reh,ehd->erd",
-        lax.all_gather(hidden, "token", axis=0, tiled=True),
-        down_w,
-        preferred_element_type=jnp.float32,
+        "reh,ehd->erd", doubled_up(hidden, "token", 0), down_w, preferred_element_type=jnp.float32
     )
     return produced.astype(jnp.bfloat16)
 

time: 167 us -> 172 us (1.030)
  other arithmetic: 7.2 us -> 13.1 us
    ppermute x0 -> x2, waiting for transfers between devices: none -> 20 us  [collected_by_bits(): other = lax.ppermute(blocks, axis, [(i, i ^ bit) for i in range(size)])]
    all_gather x1 -> x0, waiting for transfers between devices: 19.8 us -> none  [expert_block(): lax.all_gather(hidden, 'token', axis=0, tiled=True)]
    another operation x2 -> x6, other arithmetic: 1.19 us -> 6.75 us  [the longest x4 5.56 us: collected_by_bits(): both = jnp.stack([blocks, other])]
  transfers between devices with their start and end apart: 3 -> 4, of which waited for: 3 -> 4; matrix products, arithmetic and copies ran while one was open for 0% -> 1% of each run, Pallas kernels for 0% -> 0%
where the time goes in v1:
time: 172 us
  waiting for transfers between devices  82.1 us (48%)
  blocking collectives  31.9 us (19%)
  local copies, waits for them, and re-layouts  18.9 us (11%)
  between operations  13.5 us (8%)
  other arithmetic  13.1 us (8%)
  matrix products  7.25 us (4%)
  starting transfers between devices  5.08 us (3%)
    reduce_scatter x1, waiting for transfers between devices, expert_block(): lax.psum_scatter(gate_up_terms(inputs, gate_up_w).astype(jnp.bfloat16), '...  37 us
    all_to_all x1, blocking collectives, per_device(): lax.all_to_all(outgoing, 'expert', split_axis=1, concat_axis=1, tiled=True)  31.9 us
    all_to_all x1, waiting for transfers between devices, per_device(): lax.all_to_all(expert_out.reshape(local_experts, n_expert, capacity, feat...  25 us
    ppermute x2, waiting for transfers between devices, collected_by_bits(): other = lax.ppermute(blocks, axis, [(i, i ^ bit) for i in range(size)])  20 us
    dot_general x1, matrix products, gate_up_terms(): jnp.einsum('erd,edf->ref', inputs, w_gate_up, preferred_element_type=jnp....  6.28 us
    another operation x4, other arithmetic, collected_by_bits(): both = jnp.stack([blocks, other])  5.56 us
    gather x1, local copies, waits for them, and re-layouts, per_device(): jnp.take(padded, slot_table, axis=0)  5.06 us
    all_to_all x1, starting transfers between devices, per_device(): lax.all_to_all(expert_out.reshape(local_experts, n_expert, capacity, feat...  4.74 us
  transfers between devices with their start and end apart: 4, of which 4 were waited for; matrix products, arithmetic and copies ran while one was open for 1% of the time, Pallas kernels for 0%

profile of v1, /device:TPU:0, one launch (start us, length us, event | category | flops | bytes accessed | tf_op | source)
XLA Modules:
  0.0 171.8 jit_solution(9635469327165170938)
XLA Ops:
  6.5 0.0 copy-start
  6.5 0.0 reduce-scatter.2.cloned.1.call-start
  6.5 0.9 copy.33
  7.5 0.1 eq.34
  7.6 0.1 reshape.183
  7.6 0.1 reshape.185
  7.8 1.2 reduce-window.6
  8.9 0.2 slice_reduce_fusion
  9.2 0.1 fusion.9
  9.3 2.4 %scatter_custom_fusion = s32[1024]{0:T(1024)S(1)} fusion(s32[512]{0:T(512)S(1)} %bitcast.48, s32[512]{0:T(512)S(1)} %add_select_fusion.2, s32[]{:T(128)} %constant.86.clone.1), kind=kCustom, calls=%fused_computation.60 | custom fusion | bytes 4100 | tf_op jit(solution)/shard_map/scatter | solution.py:71
  11.8 0.1 broadcast_in_dim.36
  11.9 0.8 concatenate.3
  12.7 5.1 %gather_fusion = bf16[1024,512]{1,0:T(8,128)(2,1)} fusion(bf16[65,512]{1,0:T(8,128)(2,1)S(1)} %concatenate.3, s32[1024]{0:T(1024)S(1)} %fusion.15), kind=kCustom, calls=%fused_computation | custom fusion | bytes 2101248 | tf_op jit(solution)/shard_map/jit(_take)/gather | solution.py:74
  17.8 1.4 copy_select_fusion
  19.2 31.9 %all_to_all.10 = bf16[4,4,64,512]{3,2,0,1:T(8,128)(2,1)S(1)} all-to-all(bf16[4,4,64,512]{3,2,0,1:T(8,128)(2,1)S(1)} %copy_select_fusion), channel_id=1, replica_groups=mesh['groups'=2,'expert'=4,'token'=4] {'expert'}, dimensions={1} | all-to-all | bytes 2097152 | tf_op jit(solution)/shard_map/all_to_all | solution.py:77
  51.1 0.1 copy.43
  51.2 6.3 %fusion = bf16[256,4,1536]{2,0,1:T(8,128)(2,1)} fusion(bf16[4,256,512]{2,1,0:T(8,128)(2,1)S(1)} %bitcast.44, bf16[4,512,1536]{2,1,0:T(8,128)(2,1)} %param.8), kind=kOutput, calls=%fused_computation.4 | convolution fusion | flops 1612185600 | bytes 10485760 | tf_op jit(solution)/shard_map/erd,edf->ref/dot_general | solution.py:36
  57.4 0.0 reduce-scatter.2.cloned.1.call-update
  57.5 37.0 %reduce-scatter.2.cloned.1.call-done = bf16[64,4,1536]{2,0,1:T(8,128)(2,1)} async-done(((bf16[256,4,1536]{2,0,1:T(8,128)(2,1)}), bf16[64,4,1536]{2,0,1:T(8,128)(2,1)}) %reduce-scatter.2.cloned.1.call-update) | async-done | bytes 786448 | tf_op jit(solution)/shard_map/reduce_scatter | solution.py:41
  94.5 1.3 convert_element_type.29
  95.8 0.0 copy-start.1
  95.8 1.1 copy-done.1
  97.0 1.0 fusion.29
  97.9 0.0 collective-permute-start
  97.9 1.6 fusion.28
  99.5 0.5 collective-permute-done
  100.0 1.1 pad_maximum_fusion.1
  101.1 1.4 fusion.3
  102.5 0.3 collective-permute-start.1
  102.8 19.6 %collective-permute-done.1 = bf16[2,64,4,768]{3,1,2,0:T(8,128)(2,1)} collective-permute-done((bf16[2,64,4,768]{3,1,2,0:T(8,128)(2,1)}, bf16[2,64,4,768]{3,1,2,0:T(8,128)(2,1)}, u32[]{:S(2)}, u32[]{:S(2)}) %collective-permute-start.1) | collective-permute-done | bytes 786464 | tf_op jit(solution)/shard_map/ppermute | solution.py:18
  122.4 1.5 pad_maximum_fusion
  123.9 0.3 reverse_select_fusion
  124.2 0.1 copy.44
  124.3 0.0 copy-done
  124.4 1.0 convolution_convert_fusion.1
  125.3 1.1 copy.45
  126.5 0.0 copy-start.2
  126.5 4.7 %all-to-all-start.1 = ((bf16[4,4,64,512]{3,2,0,1:T(8,128)(2,1)}), bf16[4,4,64,512]{3,2,0,1:T(8,128)(2,1)}, u32[]{:S(2)}, u32[]{:S(2)}) async-start(bf16[4,4,64,512]{3,2,0,1:T(8,128)(2,1)} %copy.45), calls=%async_computation.2 | async-start | bytes 2097152 | tf_op jit(solution)/shard_map/all_to_all | solution.py:80
  131.2 0.1 reduce_sum.23
  131.3 0.0 copy-done.2
  131.3 0.1 copy.32
  131.4 0.1 compare_and_fusion
  131.5 25.0 %all-to-all-done.1 = bf16[4,4,64,512]{3,2,0,1:T(8,128)(2,1)} async-done(((bf16[4,4,64,512]{3,2,0,1:T(8,128)(2,1)}), bf16[4,4,64,512]{3,2,0,1:T(8,128)(2,1)}, u32[]{:S(2)}, u32[]{:S(2)}) %all-to-all-start.1) | async-done | bytes 1048608 | tf_op jit(solution)/shard_map/all_to_all | solution.py:80
  156.5 2.4 %copy.46 = bf16[4,4,64,512]{3,2,1,0:T(8,128)(2,1)} copy(bf16[4,4,64,512]{3,2,0,1:T(8,128)(2,1)} %all-to-all-done.1) | data formatting | bytes 2097152 | tf_op jit(solution)/shard_map/all_to_all | solution.py:80
  158.8 4.0 %gather_fusion.1 = bf16[512,512]{1,0:T(8,128)(2,1)} fusion(bf16[1024,512]{1,0:T(8,128)(2,1)} %bitcast.42, s32[1024]{0:T(1024)S(1)} %pad_clamp_fusion), kind=kCustom, calls=%fused_computation.1 | custom fusion | bytes 1050624 | tf_op jit(solution)/shard_map/jit(_take)/gather | solution.py:87
  162.9 2.1 %multiply_reduce_fusion = bf16[64,512]{1,0:T(8,128)(2,1)} fusion(bf16[512,512]{1,0:T(8,128)(2,1)} %gather_fusion.1, f32[64,8]{1,0:T(8,128)S(1)} %copy.32, pred[64,8]{1,0:T(8,128)(4,1)S(1)} %compare_and_fusion), kind=kLoop, calls=%fused_computation.10 | loop fusion | flops 1015808 | bytes 592384 | tf_op jit(solution)/shard_map/reduce_sum | solution.py:90
  (9 shorter events, 0.1 us)
Async XLA Ops:
  6.5 117.8 %copy-start = (bf16[4,768,512]{2,1,0:T(8,128)(2,1)S(1)}, bf16[4,768,512]{2,1,0:T(8,128)(2,1)}, u32[]{:S(2)}) copy-start(bf16[4,768,512]{2,1,0:T(8,128)(2,1)} %param.9) | copy-start | bytes 9437188
  6.5 88.0 %reduce-scatter.2.cloned.1.call-start = ((), (), s32[]{:S(2)}) async-start(), calls=%async_computation.3 | async-start | bytes 3932160 | tf_op jit(solution)/shard_map/reduce_scatter | solution.py:41
  95.8 1.2 copy-start.1
  97.9 2.1 %collective-permute-start = (bf16[1,64,4,768]{3,1,2,0:T(8,128)(2,1)}, bf16[1,64,4,768]{3,1,2,0:T(8,128)(2,1)}, u32[]{:S(2)}, u32[]{:S(2)}) collective-permute-start(bf16[1,64,4,768]{3,1,2,0:T(8,128)(2,1)} %fusion.29), channel_id=1, source_target_pairs={{0,1},{1,0},{2,3},{3,2},{4,5},{5,4},{6,7},{7,6},{8,9},{9,8},{10,11... | collective-permute-start | bytes 1179656 | tf_op jit(solution)/shard_map/ppermute | solution.py:18
  102.5 19.9 %collective-permute-start.1 = (bf16[2,64,4,768]{3,1,2,0:T(8,128)(2,1)}, bf16[2,64,4,768]{3,1,2,0:T(8,128)(2,1)}, u32[]{:S(2)}, u32[]{:S(2)}) collective-permute-start(bf16[2,64,4,768]{3,1,2,0:T(8,128)(2,1)} %get-tuple-element.6), channel_id=1, source_target_pairs={{0,2},{1,3},{2,0},{3,1},{4,6},{5,7},{6,4},{7,5},{8,10},{9,11},{10,... | collective-permute-start | bytes 2359304 | tf_op jit(solution)/shard_map/ppermute | solution.py:18
  126.5 4.8 %copy-start.2 = (f32[64,8]{0,1:T(8,128)S(1)}, f32[64,8]{0,1:T(8,128)}, u32[]{:S(2)}) copy-start(f32[64,8]{0,1:T(8,128)} %param.7) | copy-start | bytes 6148
  126.5 30.0 %all-to-all-start.1 = ((bf16[4,4,64,512]{3,2,0,1:T(8,128)(2,1)}), bf16[4,4,64,512]{3,2,0,1:T(8,128)(2,1)}, u32[]{:S(2)}, u32[]{:S(2)}) async-start(bf16[4,4,64,512]{3,2,0,1:T(8,128)(2,1)} %copy.45), calls=%async_computation.2 | async-start | bytes 2097152 | tf_op jit(solution)/shard_map/all_to_all | solution.py:80
Sparse Core Ops, SparseCore 0:
  57.6 36.8 reduce-scatter.1
